TPU v7x, 1024 devices: a whole 4x4x32 slice. The times are simulated.
1024 devices in a mesh: tile: 64 (over x_hi, z), func: 16 (over y, x_lo, core).
Axes of the slice: x: 4 (x_hi: 2, x_lo: 2; x = x_hi * 2 + x_lo), y: 4, z: 32, core: 2. Of those that a mesh axis runs over, the one named last changes fastest.
Arguments:
- seeds: float32 [48, 5, 2048, 128], P('func', None, 'tile'), may hold values from -6 to 6
- checkpoints: float32 [2, 5, 2048, 128], P(None, None, ('tile', 'func')), may hold values from -0.6 to 4.2, as said below
Outputs:
- adjoint_start: float32 [48, 5, 2048, 128], P('func', None, 'tile')
Inputs may be any that keep to these rules, and one draw needn't show every extreme that they name: `checkpoints`: each checkpoint cell is a state with density between 1 and 1.5, each velocity component between -0.4 and 0.4, and pressure between 1 and 1.5.
All inputs are finite; a program needn't handle non-finite values.
Results may differ from a plain program's by a relative error of at most 0.00002.
Values sent between devices are 32-bit elements; how exact they have to be, the bound alone decides.
A program may use at most 32 MiB of HBM per device.

v0:
```python
import jax
import jax.numpy as jnp
from jax import lax
from jax.sharding import PartitionSpec as P

NZ = 4
STEPS = 2


step_size = 0.3


def with_halo(cells, sides, width):
    for axis, dim in sides:
        count = lax.axis_size(axis)
        head = lax.slice_in_dim(cells, 0, width, axis=dim)
        tail = lax.slice_in_dim(cells, cells.shape[dim] - width, cells.shape[dim], axis=dim)
        cells = jnp.concatenate(
            [
                lax.ppermute(tail, axis, [(i, (i + 1) % count) for i in range(count)]),
                cells,
                lax.ppermute(head, axis, [((i + 1) % count, i) for i in range(count)]),
            ],
            axis=dim,
        )
    return cells


def trim_rows(field, depth):
    total = field.shape[-2]
    return lax.slice_in_dim(field, depth, total - depth, axis=field.ndim - 2)


def diff_trim(padded):
    inner_count = padded.shape[-2] - 4
    position = padded.ndim - 2

    def window_at(offset):
        return lax.slice_in_dim(padded, offset, offset + inner_count, axis=position)

    return (window_at(0) - window_at(4) + 8.0 * (window_at(3) - window_at(1))) / 12.0


def diff_second(field):
    return (
        jnp.roll(field, 2 * NZ, axis=-1)
        - jnp.roll(field, -2 * NZ, axis=-1)
        + 8.0 * (jnp.roll(field, -NZ, axis=-1) - jnp.roll(field, NZ, axis=-1))
    ) / 12.0


def pressure(state):
    density, mom_x, mom_y, mom_z, energy = (state[0], state[1], state[2], state[3], state[4])
    return 0.4 * (energy - (mom_x * mom_x + mom_y * mom_y + mom_z * mom_z) / (2.0 * density))


def flux_first(state):
    density, mom_x, mom_y, mom_z, energy = (state[0], state[1], state[2], state[3], state[4])
    speed = mom_x / density
    press = pressure(state)
    return jnp.stack(
        [mom_x, mom_x * speed + press, mom_y * speed, mom_z * speed, (energy + press) * speed]
    )


def flux_second(state):
    density, mom_x, mom_y, mom_z, energy = (state[0], state[1], state[2], state[3], state[4])
    speed = mom_y / density
    press = pressure(state)
    return jnp.stack(
        [mom_y, mom_x * speed, mom_y * speed + press, mom_z * speed, (energy + press) * speed]
    )


def rhs_trim(state):
    inner = trim_rows(state, 2)
    return -(diff_trim(flux_first(state)) + diff_second(flux_second(inner)))


def strip_sections(strip):
    padded = with_halo(strip, (("tile", 1),), 6)
    slope_one = rhs_trim(padded)
    section_two = trim_rows(padded, 2) + 0.5 * step_size * slope_one
    slope_two = rhs_trim(section_two)
    section_three = trim_rows(padded, 4) + 0.5 * step_size * slope_two
    slope_three = rhs_trim(section_three)
    section_four = trim_rows(padded, 6) + step_size * slope_three
    return (
        trim_rows(padded, 6),
        trim_rows(section_two, 4),
        trim_rows(section_three, 2),
        section_four,
    )


def section_pullback(state, cotangent):
    along_first = diff_trim(cotangent)
    along_second = diff_second(trim_rows(cotangent, 2))
    unused_one, pull_first = jax.vjp(flux_first, state)
    unused_two, pull_second = jax.vjp(flux_second, state)

    def apply_both(first_part, second_part):
        return pull_first(first_part)[0] + pull_second(second_part)[0]

    return jax.vmap(apply_both)(along_first, along_second)


def rimmed_pullback(state, cotangent):
    padded = with_halo(cotangent, (("tile", 2),), 2)
    return section_pullback(state, padded)


def local(seeds, checkpoints):
    adjoint = seeds
    for moment in reversed(range(STEPS)):
        strip = lax.all_gather(checkpoints[moment], "func", axis=1, tiled=True)
        section_one, section_two, section_three, section_four = strip_sections(strip)
        term_four = rimmed_pullback(section_four, step_size / 6.0 * adjoint)
        term_three = rimmed_pullback(
            section_three, step_size / 3.0 * adjoint + step_size * term_four
        )
        term_two = rimmed_pullback(
            section_two, step_size / 3.0 * adjoint + 0.5 * step_size * term_three
        )
        term_one = rimmed_pullback(
            section_one, step_size / 6.0 * adjoint + 0.5 * step_size * term_two
        )
        adjoint = adjoint + term_one + term_two + term_three + term_four
    return adjoint


def solution(mesh):
    return jax.shard_map(
        local,
        mesh=mesh,
        in_specs=(P("func", None, "tile", None), P(None, None, ("tile", "func"), None)),
        out_specs=P("func", None, "tile", None),
        check_vma=False,
    )
```

profile of v0, /device:TPU:2, one launch (start us, length us, event | category | flops | bytes accessed | tf_op | source)
XLA Modules:
  0.0 177.1 jit_solution(4910553369028365082)
XLA Ops:
  0.0 0.8 fusion.258
  0.8 29.4 %all-gather = f32[1,5,32,128]{3,0,1,2:T(1,128)S(1)} all-gather(f32[1,5,2,128]{3,0,1,2:T(1,128)S(1)} %copy.29), channel_id=2, replica_groups=mesh['tile'=64,'func'=16] {'func'}, dimensions={2}, use_global_device_ids=true | all-gather | bytes 87040 | tf_op jit(solution)/shard_map/all_gather | solution.py:116
  30.1 8.2 %collective-permute-start.3 = (f32[5,6,128]{2,1,0:T(8,128)S(1)}, f32[5,6,128]{2,1,0:T(8,128)S(1)}, u32[]{:S(2)}, u32[]{:S(2)}) collective-permute-start(f32[5,6,128]{2,1,0:T(8,128)S(1)} %get-tuple-element.450), channel_id=1, source_target_pairs={{16,0},{32,16},{48,32},{64,48},{80,64},{96,80},{112,96},{128,112},... | collective-permute-start | bytes 46088 | tf_op jit(solution)/shard_map/ppermute | solution.py:22
  38.4 1.9 %collective-permute-start.2 = (f32[5,6,128]{2,1,0:T(8,128)S(1)}, f32[5,6,128]{2,1,0:T(8,128)S(1)}, u32[]{:S(2)}, u32[]{:S(2)}) collective-permute-start(f32[5,6,128]{2,1,0:T(8,128)S(1)} %get-tuple-element.449), channel_id=1, source_target_pairs={{0,16},{16,32},{32,48},{48,64},{64,80},{80,96},{96,112},{112,128},... | collective-permute-start | bytes 46088 | tf_op jit(solution)/shard_map/ppermute | solution.py:20
  40.4 7.5 %collective-permute-start.1 = (f32[3,5,2,128]{3,2,1,0:T(2,128)S(1)}, f32[3,5,2,128]{3,2,1,0:T(2,128)S(1)}, u32[]{:S(2)}, u32[]{:S(2)}) collective-permute-start(f32[3,5,2,128]{3,2,1,0:T(2,128)S(1)} %get-tuple-element.276), channel_id=1, source_target_pairs={{16,0},{32,16},{48,32},{64,48},{80,64},{96,80},{112,96},{128,112},... | collective-permute-start | bytes 46088 | tf_op jit(solution)/shard_map/ppermute | solution.py:22
  47.9 1.9 %collective-permute-start = (f32[3,5,2,128]{3,2,1,0:T(2,128)S(1)}, f32[3,5,2,128]{3,2,1,0:T(2,128)S(1)}, u32[]{:S(2)}, u32[]{:S(2)}) collective-permute-start(f32[3,5,2,128]{3,2,1,0:T(2,128)S(1)} %get-tuple-element.275), channel_id=1, source_target_pairs={{0,16},{16,32},{32,48},{48,64},{64,80},{80,96},{96,112},{112,128},... | collective-permute-start | bytes 46088 | tf_op jit(solution)/shard_map/ppermute | solution.py:20
  49.9 20.2 %all-gather.1 = f32[1,5,32,128]{3,0,1,2:T(1,128)S(1)} all-gather(f32[1,5,2,128]{3,0,1,2:T(1,128)S(1)} %copy.30), channel_id=3, replica_groups=mesh['tile'=64,'func'=16] {'func'}, dimensions={2}, use_global_device_ids=true | all-gather | bytes 87040 | tf_op jit(solution)/shard_map/all_gather | solution.py:116
  70.0 6.9 %collective-permute-start.13 = (f32[5,6,128]{2,1,0:T(8,128)S(1)}, f32[5,6,128]{2,1,0:T(8,128)S(1)}, u32[]{:S(2)}, u32[]{:S(2)}) collective-permute-start(f32[5,6,128]{2,1,0:T(8,128)S(1)} %get-tuple-element.411), channel_id=1, source_target_pairs={{16,0},{32,16},{48,32},{64,48},{80,64},{96,80},{112,96},{128,112},... | collective-permute-start | bytes 46088 | tf_op jit(solution)/shard_map/ppermute | solution.py:22
  78.0 1.9 %collective-permute-start.12 = (f32[5,6,128]{2,1,0:T(8,128)S(1)}, f32[5,6,128]{2,1,0:T(8,128)S(1)}, u32[]{:S(2)}, u32[]{:S(2)}) collective-permute-start(f32[5,6,128]{2,1,0:T(8,128)S(1)} %get-tuple-element.410), channel_id=1, source_target_pairs={{0,16},{16,32},{32,48},{48,64},{64,80},{80,96},{96,112},{112,128},... | collective-permute-start | bytes 46088 | tf_op jit(solution)/shard_map/ppermute | solution.py:20
  83.4 3.9 %collective-permute-done.12 = f32[5,6,128]{2,1,0:T(8,128)S(1)} collective-permute-done((f32[5,6,128]{2,1,0:T(8,128)S(1)}, f32[5,6,128]{2,1,0:T(8,128)S(1)}, u32[]{:S(2)}, u32[]{:S(2)}) %collective-permute-start.12) | collective-permute-done | bytes 15392 | tf_op jit(solution)/shard_map/ppermute | solution.py:20
  89.6 3.7 %collective-permute-start.5 = (f32[3,5,2,128]{3,2,1,0:T(2,128)S(1)}, f32[3,5,2,128]{3,2,1,0:T(2,128)S(1)}, u32[]{:S(2)}, u32[]{:S(2)}) collective-permute-start(f32[3,5,2,128]{3,2,1,0:T(2,128)S(1)} %get-tuple-element.266), channel_id=1, source_target_pairs={{16,0},{32,16},{48,32},{64,48},{80,64},{96,80},{112,96},{128,112},... | collective-permute-start | bytes 46088 | tf_op jit(solution)/shard_map/ppermute | solution.py:22
  93.3 2.2 %collective-permute-start.4 = (f32[3,5,2,128]{3,2,1,0:T(2,128)S(1)}, f32[3,5,2,128]{3,2,1,0:T(2,128)S(1)}, u32[]{:S(2)}, u32[]{:S(2)}) collective-permute-start(f32[3,5,2,128]{3,2,1,0:T(2,128)S(1)} %get-tuple-element.265), channel_id=1, source_target_pairs={{0,16},{16,32},{32,48},{48,64},{64,80},{80,96},{96,112},{112,128},... | collective-permute-start | bytes 46088 | tf_op jit(solution)/shard_map/ppermute | solution.py:20
  95.8 6.7 %collective-permute-done.4 = f32[3,5,2,128]{3,2,1,0:T(2,128)S(1)} collective-permute-done((f32[3,5,2,128]{3,2,1,0:T(2,128)S(1)}, f32[3,5,2,128]{3,2,1,0:T(2,128)S(1)}, u32[]{:S(2)}, u32[]{:S(2)}) %collective-permute-start.4) | collective-permute-done | bytes 15392 | tf_op jit(solution)/shard_map/ppermute | solution.py:20
  103.6 1.9 %collective-permute-start.7 = (f32[3,5,2,128]{3,2,1,0:T(2,128)S(1)}, f32[3,5,2,128]{3,2,1,0:T(2,128)S(1)}, u32[]{:S(2)}, u32[]{:S(2)}) collective-permute-start(f32[3,5,2,128]{3,2,1,0:T(2,128)S(1)} %get-tuple-element.256), channel_id=1, source_target_pairs={{16,0},{32,16},{48,32},{64,48},{80,64},{96,80},{112,96},{128,112},... | collective-permute-start | bytes 46088 | tf_op jit(solution)/shard_map/ppermute | solution.py:22
  105.5 3.9 %collective-permute-start.6 = (f32[3,5,2,128]{3,2,1,0:T(2,128)S(1)}, f32[3,5,2,128]{3,2,1,0:T(2,128)S(1)}, u32[]{:S(2)}, u32[]{:S(2)}) collective-permute-start(f32[3,5,2,128]{3,2,1,0:T(2,128)S(1)} %get-tuple-element.255), channel_id=1, source_target_pairs={{0,16},{16,32},{32,48},{48,64},{64,80},{80,96},{96,112},{112,128},... | collective-permute-start | bytes 46088 | tf_op jit(solution)/shard_map/ppermute | solution.py:20
  109.8 5.0 %collective-permute-done.6 = f32[3,5,2,128]{3,2,1,0:T(2,128)S(1)} collective-permute-done((f32[3,5,2,128]{3,2,1,0:T(2,128)S(1)}, f32[3,5,2,128]{3,2,1,0:T(2,128)S(1)}, u32[]{:S(2)}, u32[]{:S(2)}) %collective-permute-start.6) | collective-permute-done | bytes 15392 | tf_op jit(solution)/shard_map/ppermute | solution.py:20
  115.8 1.9 %collective-permute-start.9 = (f32[3,5,2,128]{3,2,1,0:T(2,128)S(1)}, f32[3,5,2,128]{3,2,1,0:T(2,128)S(1)}, u32[]{:S(2)}, u32[]{:S(2)}) collective-permute-start(f32[3,5,2,128]{3,2,1,0:T(2,128)S(1)} %get-tuple-element.246), channel_id=1, source_target_pairs={{16,0},{32,16},{48,32},{64,48},{80,64},{96,80},{112,96},{128,112},... | collective-permute-start | bytes 46088 | tf_op jit(solution)/shard_map/ppermute | solution.py:22
  117.7 3.9 %collective-permute-start.8 = (f32[3,5,2,128]{3,2,1,0:T(2,128)S(1)}, f32[3,5,2,128]{3,2,1,0:T(2,128)S(1)}, u32[]{:S(2)}, u32[]{:S(2)}) collective-permute-start(f32[3,5,2,128]{3,2,1,0:T(2,128)S(1)} %get-tuple-element.245), channel_id=1, source_target_pairs={{0,16},{16,32},{32,48},{48,64},{64,80},{80,96},{96,112},{112,128},... | collective-permute-start | bytes 46088 | tf_op jit(solution)/shard_map/ppermute | solution.py:20
  122.0 5.0 %collective-permute-done.8 = f32[3,5,2,128]{3,2,1,0:T(2,128)S(1)} collective-permute-done((f32[3,5,2,128]{3,2,1,0:T(2,128)S(1)}, f32[3,5,2,128]{3,2,1,0:T(2,128)S(1)}, u32[]{:S(2)}, u32[]{:S(2)}) %collective-permute-start.8) | collective-permute-done | bytes 15392 | tf_op jit(solution)/shard_map/ppermute | solution.py:20
  128.1 1.9 %collective-permute-start.11 = (f32[3,5,2,128]{3,2,1,0:T(2,128)S(1)}, f32[3,5,2,128]{3,2,1,0:T(2,128)S(1)}, u32[]{:S(2)}, u32[]{:S(2)}) collective-permute-start(f32[3,5,2,128]{3,2,1,0:T(2,128)S(1)} %get-tuple-element.236), channel_id=1, source_target_pairs={{16,0},{32,16},{48,32},{64,48},{80,64},{96,80},{112,96},{128,112},... | collective-permute-start | bytes 46088 | tf_op jit(solution)/shard_map/ppermute | solution.py:22
  130.0 3.9 %collective-permute-start.10 = (f32[3,5,2,128]{3,2,1,0:T(2,128)S(1)}, f32[3,5,2,128]{3,2,1,0:T(2,128)S(1)}, u32[]{:S(2)}, u32[]{:S(2)}) collective-permute-start(f32[3,5,2,128]{3,2,1,0:T(2,128)S(1)} %get-tuple-element.235), channel_id=1, source_target_pairs={{0,16},{16,32},{32,48},{48,64},{64,80},{80,96},{96,112},{112,128},... | collective-permute-start | bytes 46088 | tf_op jit(solution)/shard_map/ppermute | solution.py:20
  134.3 5.0 %collective-permute-done.10 = f32[3,5,2,128]{3,2,1,0:T(2,128)S(1)} collective-permute-done((f32[3,5,2,128]{3,2,1,0:T(2,128)S(1)}, f32[3,5,2,128]{3,2,1,0:T(2,128)S(1)}, u32[]{:S(2)}, u32[]{:S(2)}) %collective-permute-start.10) | collective-permute-done | bytes 15392 | tf_op jit(solution)/shard_map/ppermute | solution.py:20
  140.3 1.9 %collective-permute-start.15 = (f32[3,5,2,128]{3,2,1,0:T(2,128)S(1)}, f32[3,5,2,128]{3,2,1,0:T(2,128)S(1)}, u32[]{:S(2)}, u32[]{:S(2)}) collective-permute-start(f32[3,5,2,128]{3,2,1,0:T(2,128)S(1)} %get-tuple-element.226), channel_id=1, source_target_pairs={{16,0},{32,16},{48,32},{64,48},{80,64},{96,80},{112,96},{128,112},... | collective-permute-start | bytes 46088 | tf_op jit(solution)/shard_map/ppermute | solution.py:22
  142.2 3.9 %collective-permute-start.14 = (f32[3,5,2,128]{3,2,1,0:T(2,128)S(1)}, f32[3,5,2,128]{3,2,1,0:T(2,128)S(1)}, u32[]{:S(2)}, u32[]{:S(2)}) collective-permute-start(f32[3,5,2,128]{3,2,1,0:T(2,128)S(1)} %get-tuple-element.225), channel_id=1, source_target_pairs={{0,16},{16,32},{32,48},{48,64},{64,80},{80,96},{96,112},{112,128},... | collective-permute-start | bytes 46088 | tf_op jit(solution)/shard_map/ppermute | solution.py:20
  146.5 5.0 %collective-permute-done.14 = f32[3,5,2,128]{3,2,1,0:T(2,128)S(1)} collective-permute-done((f32[3,5,2,128]{3,2,1,0:T(2,128)S(1)}, f32[3,5,2,128]{3,2,1,0:T(2,128)S(1)}, u32[]{:S(2)}, u32[]{:S(2)}) %collective-permute-start.14) | collective-permute-done | bytes 15392 | tf_op jit(solution)/shard_map/ppermute | solution.py:20
  152.5 1.9 %collective-permute-start.17 = (f32[3,5,2,128]{3,2,1,0:T(2,128)S(1)}, f32[3,5,2,128]{3,2,1,0:T(2,128)S(1)}, u32[]{:S(2)}, u32[]{:S(2)}) collective-permute-start(f32[3,5,2,128]{3,2,1,0:T(2,128)S(1)} %get-tuple-element.216), channel_id=1, source_target_pairs={{16,0},{32,16},{48,32},{64,48},{80,64},{96,80},{112,96},{128,112},... | collective-permute-start | bytes 46088 | tf_op jit(solution)/shard_map/ppermute | solution.py:22
  154.4 3.9 %collective-permute-start.16 = (f32[3,5,2,128]{3,2,1,0:T(2,128)S(1)}, f32[3,5,2,128]{3,2,1,0:T(2,128)S(1)}, u32[]{:S(2)}, u32[]{:S(2)}) collective-permute-start(f32[3,5,2,128]{3,2,1,0:T(2,128)S(1)} %get-tuple-element.215), channel_id=1, source_target_pairs={{0,16},{16,32},{32,48},{48,64},{64,80},{80,96},{96,112},{112,128},... | collective-permute-start | bytes 46088 | tf_op jit(solution)/shard_map/ppermute | solution.py:20
  158.7 5.0 %collective-permute-done.16 = f32[3,5,2,128]{3,2,1,0:T(2,128)S(1)} collective-permute-done((f32[3,5,2,128]{3,2,1,0:T(2,128)S(1)}, f32[3,5,2,128]{3,2,1,0:T(2,128)S(1)}, u32[]{:S(2)}, u32[]{:S(2)}) %collective-permute-start.16) | collective-permute-done | bytes 15392 | tf_op jit(solution)/shard_map/ppermute | solution.py:20
  164.7 1.9 %collective-permute-start.19 = (f32[3,5,2,128]{3,2,1,0:T(2,128)S(1)}, f32[3,5,2,128]{3,2,1,0:T(2,128)S(1)}, u32[]{:S(2)}, u32[]{:S(2)}) collective-permute-start(f32[3,5,2,128]{3,2,1,0:T(2,128)S(1)} %get-tuple-element.206), channel_id=1, source_target_pairs={{16,0},{32,16},{48,32},{64,48},{80,64},{96,80},{112,96},{128,112},... | collective-permute-start | bytes 46088 | tf_op jit(solution)/shard_map/ppermute | solution.py:22
  166.6 3.9 %collective-permute-start.18 = (f32[3,5,2,128]{3,2,1,0:T(2,128)S(1)}, f32[3,5,2,128]{3,2,1,0:T(2,128)S(1)}, u32[]{:S(2)}, u32[]{:S(2)}) collective-permute-start(f32[3,5,2,128]{3,2,1,0:T(2,128)S(1)} %get-tuple-element.205), channel_id=1, source_target_pairs={{0,16},{16,32},{32,48},{48,64},{64,80},{80,96},{96,112},{112,128},... | collective-permute-start | bytes 46088 | tf_op jit(solution)/shard_map/ppermute | solution.py:20
  170.9 5.0 %collective-permute-done.18 = f32[3,5,2,128]{3,2,1,0:T(2,128)S(1)} collective-permute-done((f32[3,5,2,128]{3,2,1,0:T(2,128)S(1)}, f32[3,5,2,128]{3,2,1,0:T(2,128)S(1)}, u32[]{:S(2)}, u32[]{:S(2)}) %collective-permute-start.18) | collective-permute-done | bytes 15392 | tf_op jit(solution)/shard_map/ppermute | solution.py:20
  176.2 0.9 add_add_fusion
  (223 shorter events, 14.5 us)
Async XLA Ops:
  0.0 40.3 %copy-start = (f32[3,5,32,128]{3,2,1,0:T(8,128)S(1)}, f32[3,5,32,128]{3,2,1,0:T(8,128)}, u32[]{:S(2)}) copy-start(f32[3,5,32,128]{3,2,1,0:T(8,128)} %param.2) | copy-start | bytes 737284
  30.1 47.8 %collective-permute-start.3 = (f32[5,6,128]{2,1,0:T(8,128)S(1)}, f32[5,6,128]{2,1,0:T(8,128)S(1)}, u32[]{:S(2)}, u32[]{:S(2)}) collective-permute-start(f32[5,6,128]{2,1,0:T(8,128)S(1)} %get-tuple-element.450), channel_id=1, source_target_pairs={{16,0},{32,16},{48,32},{64,48},{80,64},{96,80},{112,96},{128,112},... | collective-permute-start | bytes 46088 | tf_op jit(solution)/shard_map/ppermute | solution.py:22
  38.4 41.5 %collective-permute-start.2 = (f32[5,6,128]{2,1,0:T(8,128)S(1)}, f32[5,6,128]{2,1,0:T(8,128)S(1)}, u32[]{:S(2)}, u32[]{:S(2)}) collective-permute-start(f32[5,6,128]{2,1,0:T(8,128)S(1)} %get-tuple-element.449), channel_id=1, source_target_pairs={{0,16},{16,32},{32,48},{48,64},{64,80},{80,96},{96,112},{112,128},... | collective-permute-start | bytes 46088 | tf_op jit(solution)/shard_map/ppermute | solution.py:20
  40.4 41.9 %collective-permute-start.1 = (f32[3,5,2,128]{3,2,1,0:T(2,128)S(1)}, f32[3,5,2,128]{3,2,1,0:T(2,128)S(1)}, u32[]{:S(2)}, u32[]{:S(2)}) collective-permute-start(f32[3,5,2,128]{3,2,1,0:T(2,128)S(1)} %get-tuple-element.276), channel_id=1, source_target_pairs={{16,0},{32,16},{48,32},{64,48},{80,64},{96,80},{112,96},{128,112},... | collective-permute-start | bytes 46088 | tf_op jit(solution)/shard_map/ppermute | solution.py:22
  47.9 34.3 %collective-permute-start = (f32[3,5,2,128]{3,2,1,0:T(2,128)S(1)}, f32[3,5,2,128]{3,2,1,0:T(2,128)S(1)}, u32[]{:S(2)}, u32[]{:S(2)}) collective-permute-start(f32[3,5,2,128]{3,2,1,0:T(2,128)S(1)} %get-tuple-element.275), channel_id=1, source_target_pairs={{0,16},{16,32},{32,48},{48,64},{64,80},{80,96},{96,112},{112,128},... | collective-permute-start | bytes 46088 | tf_op jit(solution)/shard_map/ppermute | solution.py:20
  70.0 13.3 %collective-permute-start.13 = (f32[5,6,128]{2,1,0:T(8,128)S(1)}, f32[5,6,128]{2,1,0:T(8,128)S(1)}, u32[]{:S(2)}, u32[]{:S(2)}) collective-permute-start(f32[5,6,128]{2,1,0:T(8,128)S(1)} %get-tuple-element.411), channel_id=1, source_target_pairs={{16,0},{32,16},{48,32},{64,48},{80,64},{96,80},{112,96},{128,112},... | collective-permute-start | bytes 46088 | tf_op jit(solution)/shard_map/ppermute | solution.py:22
  78.0 9.3 %collective-permute-start.12 = (f32[5,6,128]{2,1,0:T(8,128)S(1)}, f32[5,6,128]{2,1,0:T(8,128)S(1)}, u32[]{:S(2)}, u32[]{:S(2)}) collective-permute-start(f32[5,6,128]{2,1,0:T(8,128)S(1)} %get-tuple-element.410), channel_id=1, source_target_pairs={{0,16},{16,32},{32,48},{48,64},{64,80},{80,96},{96,112},{112,128},... | collective-permute-start | bytes 46088 | tf_op jit(solution)/shard_map/ppermute | solution.py:20
  89.6 6.2 %collective-permute-start.5 = (f32[3,5,2,128]{3,2,1,0:T(2,128)S(1)}, f32[3,5,2,128]{3,2,1,0:T(2,128)S(1)}, u32[]{:S(2)}, u32[]{:S(2)}) collective-permute-start(f32[3,5,2,128]{3,2,1,0:T(2,128)S(1)} %get-tuple-element.266), channel_id=1, source_target_pairs={{16,0},{32,16},{48,32},{64,48},{80,64},{96,80},{112,96},{128,112},... | collective-permute-start | bytes 46088 | tf_op jit(solution)/shard_map/ppermute | solution.py:22
  93.3 9.2 %collective-permute-start.4 = (f32[3,5,2,128]{3,2,1,0:T(2,128)S(1)}, f32[3,5,2,128]{3,2,1,0:T(2,128)S(1)}, u32[]{:S(2)}, u32[]{:S(2)}) collective-permute-start(f32[3,5,2,128]{3,2,1,0:T(2,128)S(1)} %get-tuple-element.265), channel_id=1, source_target_pairs={{0,16},{16,32},{32,48},{48,64},{64,80},{80,96},{96,112},{112,128},... | collective-permute-start | bytes 46088 | tf_op jit(solution)/shard_map/ppermute | solution.py:20
  103.6 6.2 %collective-permute-start.7 = (f32[3,5,2,128]{3,2,1,0:T(2,128)S(1)}, f32[3,5,2,128]{3,2,1,0:T(2,128)S(1)}, u32[]{:S(2)}, u32[]{:S(2)}) collective-permute-start(f32[3,5,2,128]{3,2,1,0:T(2,128)S(1)} %get-tuple-element.256), channel_id=1, source_target_pairs={{16,0},{32,16},{48,32},{64,48},{80,64},{96,80},{112,96},{128,112},... | collective-permute-start | bytes 46088 | tf_op jit(solution)/shard_map/ppermute | solution.py:22
  105.5 9.2 %collective-permute-start.6 = (f32[3,5,2,128]{3,2,1,0:T(2,128)S(1)}, f32[3,5,2,128]{3,2,1,0:T(2,128)S(1)}, u32[]{:S(2)}, u32[]{:S(2)}) collective-permute-start(f32[3,5,2,128]{3,2,1,0:T(2,128)S(1)} %get-tuple-element.255), channel_id=1, source_target_pairs={{0,16},{16,32},{32,48},{48,64},{64,80},{80,96},{96,112},{112,128},... | collective-permute-start | bytes 46088 | tf_op jit(solution)/shard_map/ppermute | solution.py:20
  115.8 6.2 %collective-permute-start.9 = (f32[3,5,2,128]{3,2,1,0:T(2,128)S(1)}, f32[3,5,2,128]{3,2,1,0:T(2,128)S(1)}, u32[]{:S(2)}, u32[]{:S(2)}) collective-permute-start(f32[3,5,2,128]{3,2,1,0:T(2,128)S(1)} %get-tuple-element.246), channel_id=1, source_target_pairs={{16,0},{32,16},{48,32},{64,48},{80,64},{96,80},{112,96},{128,112},... | collective-permute-start | bytes 46088 | tf_op jit(solution)/shard_map/ppermute | solution.py:22
  117.7 9.2 %collective-permute-start.8 = (f32[3,5,2,128]{3,2,1,0:T(2,128)S(1)}, f32[3,5,2,128]{3,2,1,0:T(2,128)S(1)}, u32[]{:S(2)}, u32[]{:S(2)}) collective-permute-start(f32[3,5,2,128]{3,2,1,0:T(2,128)S(1)} %get-tuple-element.245), channel_id=1, source_target_pairs={{0,16},{16,32},{32,48},{48,64},{64,80},{80,96},{96,112},{112,128},... | collective-permute-start | bytes 46088 | tf_op jit(solution)/shard_map/ppermute | solution.py:20
  128.1 6.2 %collective-permute-start.11 = (f32[3,5,2,128]{3,2,1,0:T(2,128)S(1)}, f32[3,5,2,128]{3,2,1,0:T(2,128)S(1)}, u32[]{:S(2)}, u32[]{:S(2)}) collective-permute-start(f32[3,5,2,128]{3,2,1,0:T(2,128)S(1)} %get-tuple-element.236), channel_id=1, source_target_pairs={{16,0},{32,16},{48,32},{64,48},{80,64},{96,80},{112,96},{128,112},... | collective-permute-start | bytes 46088 | tf_op jit(solution)/shard_map/ppermute | solution.py:22
  130.0 9.2 %collective-permute-start.10 = (f32[3,5,2,128]{3,2,1,0:T(2,128)S(1)}, f32[3,5,2,128]{3,2,1,0:T(2,128)S(1)}, u32[]{:S(2)}, u32[]{:S(2)}) collective-permute-start(f32[3,5,2,128]{3,2,1,0:T(2,128)S(1)} %get-tuple-element.235), channel_id=1, source_target_pairs={{0,16},{16,32},{32,48},{48,64},{64,80},{80,96},{96,112},{112,128},... | collective-permute-start | bytes 46088 | tf_op jit(solution)/shard_map/ppermute | solution.py:20
  140.3 6.2 %collective-permute-start.15 = (f32[3,5,2,128]{3,2,1,0:T(2,128)S(1)}, f32[3,5,2,128]{3,2,1,0:T(2,128)S(1)}, u32[]{:S(2)}, u32[]{:S(2)}) collective-permute-start(f32[3,5,2,128]{3,2,1,0:T(2,128)S(1)} %get-tuple-element.226), channel_id=1, source_target_pairs={{16,0},{32,16},{48,32},{64,48},{80,64},{96,80},{112,96},{128,112},... | collective-permute-start | bytes 46088 | tf_op jit(solution)/shard_map/ppermute | solution.py:22
  142.2 9.2 %collective-permute-start.14 = (f32[3,5,2,128]{3,2,1,0:T(2,128)S(1)}, f32[3,5,2,128]{3,2,1,0:T(2,128)S(1)}, u32[]{:S(2)}, u32[]{:S(2)}) collective-permute-start(f32[3,5,2,128]{3,2,1,0:T(2,128)S(1)} %get-tuple-element.225), channel_id=1, source_target_pairs={{0,16},{16,32},{32,48},{48,64},{64,80},{80,96},{96,112},{112,128},... | collective-permute-start | bytes 46088 | tf_op jit(solution)/shard_map/ppermute | solution.py:20
  152.5 6.2 %collective-permute-start.17 = (f32[3,5,2,128]{3,2,1,0:T(2,128)S(1)}, f32[3,5,2,128]{3,2,1,0:T(2,128)S(1)}, u32[]{:S(2)}, u32[]{:S(2)}) collective-permute-start(f32[3,5,2,128]{3,2,1,0:T(2,128)S(1)} %get-tuple-element.216), channel_id=1, source_target_pairs={{16,0},{32,16},{48,32},{64,48},{80,64},{96,80},{112,96},{128,112},... | collective-permute-start | bytes 46088 | tf_op jit(solution)/shard_map/ppermute | solution.py:22
  154.4 9.2 %collective-permute-start.16 = (f32[3,5,2,128]{3,2,1,0:T(2,128)S(1)}, f32[3,5,2,128]{3,2,1,0:T(2,128)S(1)}, u32[]{:S(2)}, u32[]{:S(2)}) collective-permute-start(f32[3,5,2,128]{3,2,1,0:T(2,128)S(1)} %get-tuple-element.215), channel_id=1, source_target_pairs={{0,16},{16,32},{32,48},{48,64},{64,80},{80,96},{96,112},{112,128},... | collective-permute-start | bytes 46088 | tf_op jit(solution)/shard_map/ppermute | solution.py:20
  164.7 6.2 %collective-permute-start.19 = (f32[3,5,2,128]{3,2,1,0:T(2,128)S(1)}, f32[3,5,2,128]{3,2,1,0:T(2,128)S(1)}, u32[]{:S(2)}, u32[]{:S(2)}) collective-permute-start(f32[3,5,2,128]{3,2,1,0:T(2,128)S(1)} %get-tuple-element.206), channel_id=1, source_target_pairs={{16,0},{32,16},{48,32},{64,48},{80,64},{96,80},{112,96},{128,112},... | collective-permute-start | bytes 46088 | tf_op jit(solution)/shard_map/ppermute | solution.py:22
  166.6 9.2 %collective-permute-start.18 = (f32[3,5,2,128]{3,2,1,0:T(2,128)S(1)}, f32[3,5,2,128]{3,2,1,0:T(2,128)S(1)}, u32[]{:S(2)}, u32[]{:S(2)}) collective-permute-start(f32[3,5,2,128]{3,2,1,0:T(2,128)S(1)} %get-tuple-element.205), channel_id=1, source_target_pairs={{0,16},{16,32},{32,48},{48,64},{64,80},{80,96},{96,112},{112,128},... | collective-permute-start | bytes 46088 | tf_op jit(solution)/shard_map/ppermute | solution.py:20
where the time goes:
time: 178 us; the launch traced here: 177 us
  starting transfers between devices  69.3 us (39%)
  blocking collectives  49.5 us (28%)
  waiting for transfers between devices  40.4 us (23%)
  other arithmetic  8.92 us (5%)
  local copies, waits for them, and re-layouts  7.2 us (4%)
    all_gather x2, blocking collectives, local(): strip = lax.all_gather(checkpoints[moment], 'func', axis=1, tiled=True)  49.5 us
    ppermute x10, waiting for transfers between devices, with_halo(): lax.ppermute(tail, axis, [(i, (i + 1) % count) for i in range(count)])  40.4 us
    ppermute x10, starting transfers between devices, with_halo(): lax.ppermute(head, axis, [((i + 1) % count, i) for i in range(count)])  37.9 us
    ppermute x10, starting transfers between devices, with_halo(): lax.ppermute(tail, axis, [(i, (i + 1) % count) for i in range(count)])  31.5 us
  transfers between devices with their start and end apart: 20, of which 8 were waited for; matrix products, arithmetic and copies ran while one was open for 4% of the time, Pallas kernels for 0%

commit v1 on v0

v1 whole, which is shorter than its diff:
```python
import functools

import jax
import jax.numpy as jnp
from jax import lax
from jax.experimental import pallas as pl
from jax.experimental.pallas import tpu as pltpu
from jax.sharding import PartitionSpec as P

NZ = 4
H = 0.3
L = 128
ROWS = 80
EDGE = 24
DEEP = (12, 20)
MESH = pl.DeviceIdType.MESH


def stencil_y(a):
    far = pltpu.roll(a, 2 * NZ, 1) - pltpu.roll(a, L - 2 * NZ, 1)
    near = pltpu.roll(a, L - NZ, 1) - pltpu.roll(a, NZ, 1)
    return far + 8.0 * near


def rowsat(lo, t, shift=0):
    return pl.ds(lo + shift + 8 * t, 8)


def loop(n, f, u):
    def step(i, c):
        for j in range(u):
            t = u * i + j
            if n % u:
                t = jnp.minimum(t, n - 1)
            f(t)
        return c

    lax.fori_loop(0, -(-n // u), step, 0)


def forward(load, u0, fx, base, coef, edge):
    scale = (0.5 * H / 12.0, 0.5 * H / 12.0, H / 12.0)

    def phase(k, lo, n):
        def tile(t):
            r = rowsat(lo, t)
            if k == 0:
                u = [load(c, lo, t) for c in range(5)]
                for c in range(5):
                    u0[c, r, :] = u[c]
            else:
                src, cst, u = fx.at[(k - 1) % 2], -scale[k - 1], []
                for c in range(5):
                    d = (src[c, rowsat(lo, t, -2), :] - src[c, rowsat(lo, t, 2), :]) + 8.0 * (
                        src[c, rowsat(lo, t, 1), :] - src[c, rowsat(lo, t, -1), :]
                    )
                    u.append(base[(k - 1) % 2, c, r, :] + cst * d)
            rho, mx, my, mz, en = u
            inv = 1.0 / rho
            vx, vy, vz = mx * inv, my * inv, mz * inv
            kin2 = mx * vx + my * vy + mz * vz
            p = 0.4 * (en - 0.5 * kin2)
            ep = en + p
            coef[k, 0, r, :] = vx
            coef[k, 1, r, :] = vy
            coef[k, 2, r, :] = vz
            coef[k, 3, r, :] = ep * inv
            coef[k, 4, r, :] = 0.5 * (kin2 * inv)
            if k < 3:
                fx[k % 2, 0, r, :] = mx
                fx[k % 2, 1, r, :] = mx * vx + p
                fx[k % 2, 2, r, :] = my * vx
                fx[k % 2, 3, r, :] = mz * vx
                fx[k % 2, 4, r, :] = ep * vx
                fy = (my, mx * vy, my * vy + p, mz * vy, ep * vy)
                start = u if k == 0 else [u0[c, r, :] for c in range(5)]
                for c in range(5):
                    base[k % 2, c, r, :] = start[c] - scale[k] * stencil_y(fy[c])

        loop(n, tile, 3)

    for k in range(4):
        lo = edge + 2 * k
        phase(k, lo, -(-(ROWS - 2 * lo) // 8))


def pull(w, f, coef, lo, t):
    a, b, mid = [], [], []
    for c in range(5):
        v = w[f, c, rowsat(lo, t), :]
        mid.append(v)
        a.append(
            (w[f, c, rowsat(lo, t, -2), :] - w[f, c, rowsat(lo, t, 2), :])
            + 8.0 * (w[f, c, rowsat(lo, t, 1), :] - w[f, c, rowsat(lo, t, -1), :])
        )
        b.append(stencil_y(v))
    vx, vy, vz, en, kin = coef
    s = a[1] * vx + a[2] * vy + a[3] * vz + a[4] * en
    q = b[1] * vx + b[2] * vy + b[3] * vz + b[4] * en
    e4 = a[4] * vx + b[4] * vy
    g = 0.4 * (a[1] + b[2] + e4)
    out = (
        kin * g - s * vx - q * vy,
        a[0] + s + a[1] * vx + b[1] * vy - g * vx,
        b[0] + q + a[2] * vx + b[2] * vy - g * vy,
        a[3] * vx + b[3] * vy - g * vz,
        e4 + g,
    )
    return mid, out


def backward(adj, w3, w2, w1, coef, first, store):
    near = 3.0 * H / 72.0
    plan = ((3, adj, w3, near), (2, w3, w2, near), (1, w2, w1, 2.0 * near), (0, w1, None, H / 72.0))
    for place, (k, src, dst, cst) in enumerate(plan):
        lo = first + 2 * place

        def tile(t, k=k, src=src, dst=dst, cst=cst, lo=lo):
            r = rowsat(lo, t)
            c5 = [coef[k, c, r, :] for c in range(5)]
            for f in range(3):
                mid, out = pull(src, f, c5, lo, t)
                for c in range(5):
                    start = mid[c] if k == 3 else adj[f, c, r, :]
                    if dst is not None:
                        dst[f, c, r, :] = start + cst * out[c]
                    else:
                        mix = (w3[f, c, r, :] + mid[c]) + 2.0 * w2[f, c, r, :] - start
                        store(f, c, lo, t, mix * (1.0 / 3.0) + cst * out[c])

        loop(-(-(ROWS - 2 * lo) // 8), tile, 1)


def kernel(tiles, funcs, seeds, chk, out, u0, fx, base, coef, adj, w3, w2, w1, st, own_sem, g_send, g_recv, z_send, z_recv):
    tile, func = lax.axis_index("tile"), lax.axis_index("func")
    up, down = lax.rem(tile + 1, tiles), lax.rem(tile + tiles - 1, tiles)

    def peer(d):
        return lax.rem(func + d, funcs)

    barrier = pltpu.get_barrier_semaphore()
    for d in range(1, funcs):
        pl.semaphore_signal(barrier, inc=1, device_id=(tile, peer(d)), device_id_type=MESH)
    for t in (up, down):
        pl.semaphore_signal(barrier, inc=1, device_id=(t, func), device_id_type=MESH)

    own_seeds = pltpu.make_async_copy(seeds, adj.at[:, :, pl.ds(EDGE, 32), :], own_sem.at[0])
    own_seeds.start()
    mine = EDGE // 2 + func
    own_state = [pltpu.make_async_copy(chk.at[s], st.at[s, :, mine], own_sem.at[1 + s]) for s in range(2)]
    for s in (1, 0):
        own_state[s].start()
    pl.semaphore_wait(barrier, funcs + 1)

    gather = [[], []]
    for s in (1, 0):
        for d in range(1, funcs):
            gather[s].append(
                pltpu.make_async_remote_copy(
                    src_ref=chk.at[s],
                    dst_ref=st.at[s, :, mine],
                    send_sem=g_send.at[s, d],
                    recv_sem=g_recv.at[s, d],
                    device_id=(tile, peer(d)),
                    device_id_type=MESH,
                )
            )
    def across(src, dst, slot, to):
        return pltpu.make_async_remote_copy(
            src_ref=src, dst_ref=dst, send_sem=z_send.at[slot], recv_sem=z_recv.at[slot],
            device_id=(to, func), device_id_type=MESH,
        )

    halo = [
        across(seeds.at[:, :, pl.ds(16, 16), :], adj.at[:, :, pl.ds(EDGE - 16, 16), :], 0, up),
        across(seeds.at[:, :, pl.ds(0, 16), :], adj.at[:, :, pl.ds(EDGE + 32, 16), :], 1, down),
    ]
    for copy in gather[1] + gather[0] + halo:
        copy.start()

    rims = [[], []]
    for s in (1, 0):
        n, lo, hi = DEEP[s] // 2, EDGE // 2, EDGE // 2 + 16
        own_state[s].wait()
        for copy in gather[s]:
            copy.wait_recv()
        rims[s] = [
            across(st.at[s, :, pl.ds(hi - n, n)], st.at[s, :, pl.ds(lo - n, n)], 2 + 2 * s, up),
            across(st.at[s, :, pl.ds(lo, n)], st.at[s, :, pl.ds(hi, n)], 3 + 2 * s, down),
        ]
        for copy in rims[s]:
            copy.start()

    def load(s):
        return lambda c, lo, t: st[s, c, pl.ds(lo // 2 + 4 * t, 4), :, :].reshape(8, L)

    for copy in rims[1]:
        copy.wait_recv()
    forward(load(1), u0, fx, base, coef, EDGE - DEEP[1])
    own_seeds.wait()
    for copy in halo:
        copy.wait_recv()

    def keep(f, c, lo, t, v):
        adj[f, c, rowsat(lo, t), :] = v

    backward(adj, w3, w2, w1, coef, EDGE - 14, keep)
    for copy in rims[0]:
        copy.wait_recv()
    forward(load(0), u0, fx, base, coef, EDGE - DEEP[0])

    def finish(f, c, lo, t, v):
        out[f, c, pl.ds(lo - EDGE + 8 * t, 8), :] = v

    backward(adj, w3, w2, w1, coef, EDGE - 6, finish)
    for copy in gather[1] + gather[0] + halo + rims[1] + rims[0]:
        copy.wait_send()


def solution(mesh):
    tiles, funcs = mesh.shape["tile"], mesh.shape["func"]

    def local(seeds, checkpoints):
        field = pltpu.VMEM((3, 5, ROWS, L), jnp.float32)
        return pl.pallas_call(
            functools.partial(kernel, tiles, funcs),
            out_shape=jax.ShapeDtypeStruct(seeds.shape, jnp.float32),
            in_specs=[pl.BlockSpec(memory_space=pl.ANY)] * 2,
            out_specs=pl.BlockSpec(memory_space=pltpu.VMEM),
            scratch_shapes=[
                pltpu.VMEM((5, ROWS, L), jnp.float32),
                pltpu.VMEM((2, 5, ROWS, L), jnp.float32),
                pltpu.VMEM((2, 5, ROWS, L), jnp.float32),
                pltpu.VMEM((4, 5, ROWS, L), jnp.float32),
                field,
                field,
                field,
                field,
                pltpu.VMEM((2, 5, ROWS // 2, 2, L), jnp.float32),
                pltpu.SemaphoreType.DMA((3,)),
                pltpu.SemaphoreType.DMA((2, 16)),
                pltpu.SemaphoreType.DMA((2, 16)),
                pltpu.SemaphoreType.DMA((6,)),
                pltpu.SemaphoreType.DMA((6,)),
            ],
            compiler_params=pltpu.CompilerParams(
                collective_id=0, has_side_effects=True, vmem_limit_bytes=16 * 2**20
            ),
        )(seeds, checkpoints)

    return jax.shard_map(
        local,
        mesh=mesh,
        in_specs=(P("func", None, "tile", None), P(None, None, ("tile", "func"), None)),
        out_specs=P("func", None, "tile", None),
        check_vma=False,
    )
```

time: 178 us -> 45.8 us (0.26)
  the two profiles are of different devices: /device:TPU:2 before, /device:TPU:1 now
where the time goes in v1:
time: 45.8 us; the launch traced here: 45.6 us
  Pallas kernels  43.2 us (94%)
  local copies, waits for them, and re-layouts  2.34 us (5%)
    pallas_call x1, Pallas kernels, local(): pl.pallas_call(functools.partial(kernel, tiles, funcs), out_shape=jax.Sha...  43.2 us
    unnamed x5, local copies, waits for them, and re-layouts  2.34 us

profile of v1, /device:TPU:1, one launch (start us, length us, event | category | flops | bytes accessed | tf_op | source)
XLA Modules:
  0.0 45.6 jit_solution(13419498229901468948)
XLA Ops:
  0.0 0.0 copy-start
  0.0 0.9 %copy-done = f32[3,5,32,128]{3,2,1,0:T(8,128)S(1)} copy-done((f32[3,5,32,128]{3,2,1,0:T(8,128)S(1)}, f32[3,5,32,128]{3,2,1,0:T(8,128)}, u32[]{:S(2)}) %copy-start) | copy-done | bytes 245784
  0.9 0.0 copy-start.1
  0.9 0.7 %copy-done.1 = f32[2,5,2,128]{3,2,1,0:T(2,128)S(1)} copy-done((f32[2,5,2,128]{3,2,1,0:T(2,128)S(1)}, f32[2,5,2,128]{3,2,1,0:T(2,128)}, u32[]{:S(2)}) %copy-start.1) | copy-done | bytes 10264
  1.6 43.2 %shard_map.28 = f32[3,5,32,128]{3,2,1,0:T(8,128)S(1)} custom-call(f32[3,5,32,128]{3,2,1,0:T(8,128)S(1)} %copy-done, f32[2,5,2,128]{3,2,1,0:T(2,128)S(1)} %copy-done.1), custom_call_target="tpu_custom_call" | custom-call | tf_op jit(solution)/shard_map/pallas_call | solution.py:225
  44.9 0.7 %copy.4 = f32[3,5,32,128]{3,2,1,0:T(8,128)} copy(f32[3,5,32,128]{3,2,1,0:T(8,128)S(1)} %shard_map.28) | data formatting | bytes 491520
Async XLA Ops:
  0.0 0.9 %copy-start = (f32[3,5,32,128]{3,2,1,0:T(8,128)S(1)}, f32[3,5,32,128]{3,2,1,0:T(8,128)}, u32[]{:S(2)}) copy-start(f32[3,5,32,128]{3,2,1,0:T(8,128)} %seeds.1) | copy-start | bytes 737284
  0.9 0.7 %copy-start.1 = (f32[2,5,2,128]{3,2,1,0:T(2,128)S(1)}, f32[2,5,2,128]{3,2,1,0:T(2,128)}, u32[]{:S(2)}) copy-start(f32[2,5,2,128]{3,2,1,0:T(2,128)} %chk.1) | copy-start | bytes 30724

commit v2 on v1

v2 whole, which is shorter than its diff:
```python
import functools

import jax
import jax.numpy as jnp
from jax import lax
from jax.experimental import pallas as pl
from jax.experimental.pallas import tpu as pltpu
from jax.sharding import PartitionSpec as P

NZ = 4
H = 0.3
L = 128
ROWS = 80
EDGE = 24
DEEP = (12, 20)
MESH = pl.DeviceIdType.MESH


def stencil_y(a):
    far = pltpu.roll(a, 2 * NZ, 1) - pltpu.roll(a, L - 2 * NZ, 1)
    near = pltpu.roll(a, L - NZ, 1) - pltpu.roll(a, NZ, 1)
    return far + 8.0 * near


def rowsat(row, shift=0):
    return pl.ds(row + shift, 8)


def sweep(lo, hi, f, u):
    n = (hi - lo + 7) // 8

    def step(i, c):
        for j in range(u):
            f(jnp.minimum(lo + 8 * (u * i + j), hi - 8))
        return c

    lax.fori_loop(0, (n + u - 1) // u, step, 0)


def forward(load, u0, fx, base, coef, span):
    scale = (0.5 * H / 12.0, 0.5 * H / 12.0, H / 12.0)

    def phase(k):
        def tile(row):
            r = rowsat(row)
            if k == 0:
                u = [load(c, row) for c in range(5)]
                for c in range(5):
                    u0[c, r, :] = u[c]
            else:
                src, cst, u = fx[k - 1], -scale[k - 1], []
                for c in range(5):
                    d = (src[c, rowsat(row, -2), :] - src[c, rowsat(row, 2), :]) + 8.0 * (
                        src[c, rowsat(row, 1), :] - src[c, rowsat(row, -1), :]
                    )
                    u.append(base[k - 1][c, r, :] + cst * d)
            rho, mx, my, mz, en = u
            inv = 1.0 / rho
            vx, vy, vz = mx * inv, my * inv, mz * inv
            kin2 = mx * vx + my * vy + mz * vz
            p = 0.4 * (en - 0.5 * kin2)
            ep = en + p
            coef[k, 0, r, :] = vx
            coef[k, 1, r, :] = vy
            coef[k, 2, r, :] = vz
            coef[k, 3, r, :] = ep * inv
            coef[k, 4, r, :] = 0.5 * (kin2 * inv)
            if k < 3:
                fx[k][0, r, :] = mx
                fx[k][1, r, :] = mx * vx + p
                fx[k][2, r, :] = my * vx
                fx[k][3, r, :] = mz * vx
                fx[k][4, r, :] = ep * vx
                fy = (my, mx * vy, my * vy + p, mz * vy, ep * vy)
                start = u if k == 0 else [u0[c, r, :] for c in range(5)]
                for c in range(5):
                    base[k][c, r, :] = start[c] - scale[k] * stencil_y(fy[c])

        lo, hi = span(k)
        sweep(lo, hi, tile, 3)

    for k in range(4):
        phase(k)


def pull(w, f, coef, row):
    a, b, mid = [], [], []
    for c in range(5):
        v = w[f, c, rowsat(row), :]
        mid.append(v)
        a.append(
            (w[f, c, rowsat(row, -2), :] - w[f, c, rowsat(row, 2), :])
            + 8.0 * (w[f, c, rowsat(row, 1), :] - w[f, c, rowsat(row, -1), :])
        )
        b.append(stencil_y(v))
    vx, vy, vz, en, kin = coef
    s = a[1] * vx + a[2] * vy + a[3] * vz + a[4] * en
    q = b[1] * vx + b[2] * vy + b[3] * vz + b[4] * en
    e4 = a[4] * vx + b[4] * vy
    g = 0.4 * (a[1] + b[2] + e4)
    out = (
        kin * g - s * vx - q * vy,
        a[0] + s + a[1] * vx + b[1] * vy - g * vx,
        b[0] + q + a[2] * vx + b[2] * vy - g * vy,
        a[3] * vx + b[3] * vy - g * vz,
        e4 + g,
    )
    return mid, out


def backward(adj, w3, w2, w1, coef, span, store):
    near = 3.0 * H / 72.0
    plan = ((3, adj, w3, near), (2, w3, w2, near), (1, w2, w1, 2.0 * near), (0, w1, None, H / 72.0))
    for place, (k, src, dst, cst) in enumerate(plan):

        def tile(row, k=k, src=src, dst=dst, cst=cst):
            r = rowsat(row)
            c5 = [coef[k, c, r, :] for c in range(5)]
            for f in range(3):
                mid, out = pull(src, f, c5, row)
                for c in range(5):
                    start = mid[c] if k == 3 else adj[f, c, r, :]
                    if dst is not None:
                        dst[f, c, r, :] = start + cst * out[c]
                    else:
                        mix = (w3[f, c, r, :] + mid[c]) + 2.0 * w2[f, c, r, :] - start
                        store(f, c, row, mix * (1.0 / 3.0) + cst * out[c])

        lo, hi = span(place)
        sweep(lo, hi, tile, 1)


def kernel(tiles, funcs, seeds, chk, out, *scratch):
    u0, fx, base = scratch[0:2], (scratch[2:5], scratch[5:8]), (scratch[8:11], scratch[11:14])
    coef, fields = scratch[14:16], scratch[16:24]
    st, own_sem, g_send, g_recv, z_send, z_recv = scratch[24:]
    tile, func = lax.axis_index("tile"), lax.axis_index("func")
    up, down = lax.rem(tile + 1, tiles), lax.rem(tile + tiles - 1, tiles)
    adj = fields[0]

    def peer(d):
        return lax.rem(func + d, funcs)

    barrier = pltpu.get_barrier_semaphore()
    for d in range(1, funcs):
        pl.semaphore_signal(barrier, inc=1, device_id=(tile, peer(d)), device_id_type=MESH)
    for t in (up, down):
        pl.semaphore_signal(barrier, inc=1, device_id=(t, func), device_id_type=MESH)

    mine = EDGE // 2 + func
    own_state = [pltpu.make_async_copy(chk.at[s], st.at[s, :, mine], own_sem.at[1 + s]) for s in range(2)]
    for s in (1, 0):
        own_state[s].start()
    own_seeds = pltpu.make_async_copy(seeds, adj.at[:, :, pl.ds(EDGE, 32), :], own_sem.at[0])
    own_seeds.start()
    pl.semaphore_wait(barrier, funcs + 1)

    gather = [
        [
            pltpu.make_async_remote_copy(
                src_ref=chk.at[s],
                dst_ref=st.at[s, :, mine],
                send_sem=g_send.at[s, d],
                recv_sem=g_recv.at[s, d],
                device_id=(tile, peer(d)),
                device_id_type=MESH,
            )
            for d in range(1, funcs)
        ]
        for s in range(2)
    ]

    def across(src, dst, slot, to):
        return pltpu.make_async_remote_copy(
            src_ref=src, dst_ref=dst, send_sem=z_send.at[slot], recv_sem=z_recv.at[slot],
            device_id=(to, func), device_id_type=MESH,
        )

    lo, hi = EDGE // 2, EDGE // 2 + 16
    rims = [
        (
            across(st.at[s, :, pl.ds(hi - n, n)], st.at[s, :, pl.ds(lo - n, n)], 2 + 2 * s, up),
            across(st.at[s, :, pl.ds(lo, n)], st.at[s, :, pl.ds(hi, n)], 3 + 2 * s, down),
        )
        for s, n in enumerate((DEEP[0] // 2, DEEP[1] // 2))
    ]
    halo = (
        across(seeds.at[:, :, pl.ds(16, 16), :], adj.at[:, :, pl.ds(EDGE - 16, 16), :], 0, up),
        across(seeds.at[:, :, pl.ds(0, 16), :], adj.at[:, :, pl.ds(EDGE + 32, 16), :], 1, down),
    )
    for copy in gather[1]:
        copy.start()
    for copy in halo:
        copy.start()

    def relay(s):
        own_state[s].wait()
        for copy in gather[s]:
            copy.wait_recv()
        for copy in rims[s]:
            copy.start()

    relay(1)
    for copy in gather[0]:
        copy.start()
    own_seeds.wait()

    def load(s):
        return lambda c, row: st[s, c, pl.ds(row // 2, 4), :, :].reshape(8, L)

    def part(g, carry):
        def only(want, copies):
            @pl.when(g == want)
            def _():
                for copy in copies:
                    copy.wait_recv()

        def region(below, above, low):
            return jnp.where(g == 0, EDGE + low, EDGE + below), jnp.where(g == 0, EDGE + above, EDGE + low)

        def sections(s):
            n = DEEP[s]
            return lambda k: region(2 * k - n, 32 + n - 2 * k, 2 * k)

        def stages(first):
            return lambda place: region(-16 + 2 * (first + place), 48 - 2 * (first + place), 4 + 2 * (first + place))

        only(0, (rims[1][1],))
        only(1, (rims[1][0], halo[0]))
        forward(load(1), u0[1], fx[1], base[1], coef[1], sections(1))

        @pl.when(g == 0)
        def _():
            relay(0)

        only(0, (halo[1],))

        def keep(f, c, row, v):
            fields[4][f, c, rowsat(row), :] = v

        backward(*fields[0:4], coef[1], stages(1), keep)
        only(0, (rims[0][1],))
        only(1, (rims[0][0],))
        forward(load(0), u0[0], fx[0], base[0], coef[0], sections(0))

        def finish(f, c, row, v):
            out[f, c, pl.ds(row - EDGE, 8), :] = v

        backward(*fields[4:8], coef[0], stages(5), finish)
        return carry

    lax.fori_loop(0, 2, part, 0)
    for copies in (*gather, halo, *rims):
        for copy in copies:
            copy.wait_send()


def solution(mesh):
    tiles, funcs = mesh.shape["tile"], mesh.shape["func"]

    def local(seeds, checkpoints):
        state = pltpu.VMEM((5, ROWS, L), jnp.float32)
        field = pltpu.VMEM((3, 5, ROWS, L), jnp.float32)
        return pl.pallas_call(
            functools.partial(kernel, tiles, funcs),
            out_shape=jax.ShapeDtypeStruct(seeds.shape, jnp.float32),
            in_specs=[pl.BlockSpec(memory_space=pltpu.HBM)] * 2,
            out_specs=pl.BlockSpec(memory_space=pltpu.VMEM),
            scratch_shapes=[state] * 14
            + [pltpu.VMEM((4, 5, ROWS, L), jnp.float32)] * 2
            + [field] * 8
            + [
                pltpu.VMEM((2, 5, ROWS // 2, 2, L), jnp.float32),
                pltpu.SemaphoreType.DMA((3,)),
                pltpu.SemaphoreType.DMA((2, 16)),
                pltpu.SemaphoreType.DMA((2, 16)),
                pltpu.SemaphoreType.DMA((6,)),
                pltpu.SemaphoreType.DMA((6,)),
            ],
            compiler_params=pltpu.CompilerParams(
                collective_id=0, has_side_effects=True, vmem_limit_bytes=16 * 2**20
            ),
        )(seeds, checkpoints)

    return jax.shard_map(
        local,
        mesh=mesh,
        in_specs=(P("func", None, "tile", None), P(None, None, ("tile", "func"), None)),
        out_specs=P("func", None, "tile", None),
        check_vma=False,
    )
```

time: 45.8 us -> 45.9 us (level)
  no operation moved by 1% of the time
where the time goes in v2:
time: 45.9 us; the launch traced here: 45.7 us
  Pallas kernels  43.4 us (95%)
  local copies, waits for them, and re-layouts  2.34 us (5%)
    pallas_call x1, Pallas kernels, local(): pl.pallas_call(functools.partial(kernel, tiles, funcs), out_shape=jax.Sha...  43.4 us
    unnamed x5, local copies, waits for them, and re-layouts  2.34 us

profile of v2, /device:TPU:1, one launch (start us, length us, event | category | flops | bytes accessed | tf_op | source)
XLA Modules:
  0.0 45.7 jit_solution(9460300920947593771)
XLA Ops:
  0.0 0.0 copy-start
  0.0 0.9 %copy-done = f32[3,5,32,128]{3,2,1,0:T(8,128)S(1)} copy-done((f32[3,5,32,128]{3,2,1,0:T(8,128)S(1)}, f32[3,5,32,128]{3,2,1,0:T(8,128)}, u32[]{:S(2)}) %copy-start) | copy-done | bytes 245784
  0.9 0.0 copy-start.1
  0.9 0.7 %copy-done.1 = f32[2,5,2,128]{3,2,1,0:T(2,128)S(1)} copy-done((f32[2,5,2,128]{3,2,1,0:T(2,128)S(1)}, f32[2,5,2,128]{3,2,1,0:T(2,128)}, u32[]{:S(2)}) %copy-start.1) | copy-done | bytes 10264
  1.6 43.4 %shard_map.28 = f32[3,5,32,128]{3,2,1,0:T(8,128)S(1)} custom-call(f32[3,5,32,128]{3,2,1,0:T(8,128)S(1)} %copy-done, f32[2,5,2,128]{3,2,1,0:T(2,128)S(1)} %copy-done.1), custom_call_target="tpu_custom_call" | custom-call | tf_op jit(solution)/shard_map/pallas_call | solution.py:264
  45.0 0.7 %copy.4 = f32[3,5,32,128]{3,2,1,0:T(8,128)} copy(f32[3,5,32,128]{3,2,1,0:T(8,128)S(1)} %shard_map.28) | data formatting | bytes 491520
Async XLA Ops:
  0.0 0.9 %copy-start = (f32[3,5,32,128]{3,2,1,0:T(8,128)S(1)}, f32[3,5,32,128]{3,2,1,0:T(8,128)}, u32[]{:S(2)}) copy-start(f32[3,5,32,128]{3,2,1,0:T(8,128)} %seeds.1) | copy-start | bytes 737284
  0.9 0.7 %copy-start.1 = (f32[2,5,2,128]{3,2,1,0:T(2,128)S(1)}, f32[2,5,2,128]{3,2,1,0:T(2,128)}, u32[]{:S(2)}) copy-start(f32[2,5,2,128]{3,2,1,0:T(2,128)} %chk.1) | copy-start | bytes 30724

commit v3 on v2

--- a/solution.py
+++ b/solution.py
@@ -133,10 +133,12 @@
 def kernel(tiles, funcs, seeds, chk, out, *scratch):
     u0, fx, base = scratch[0:2], (scratch[2:5], scratch[5:8]), (scratch[8:11], scratch[11:14])
     coef, fields = scratch[14:16], scratch[16:24]
-    st, own_sem, g_send, g_recv, z_send, z_recv = scratch[24:]
+    st, own_sem, g_send, g_recv, z_send, z_recv, entered = scratch[24:]
     tile, func = lax.axis_index("tile"), lax.axis_index("func")
     up, down = lax.rem(tile + 1, tiles), lax.rem(tile + tiles - 1, tiles)
     adj = fields[0]
+    bottom = lax.rem(tile, tiles // 2) == 0
+    top = lax.rem(tile, tiles // 2) == tiles // 2 - 1
 
     def peer(d):
         return lax.rem(func + d, funcs)
@@ -144,8 +146,12 @@
     barrier = pltpu.get_barrier_semaphore()
     for d in range(1, funcs):
         pl.semaphore_signal(barrier, inc=1, device_id=(tile, peer(d)), device_id_type=MESH)
-    for t in (up, down):
-        pl.semaphore_signal(barrier, inc=1, device_id=(t, func), device_id_type=MESH)
+    pl.semaphore_signal(barrier, inc=1, device_id=(down, func), device_id_type=MESH)
+
+    @pl.when(jnp.logical_not(top))
+    def _():
+        pl.semaphore_signal(barrier, inc=1, device_id=(up, func), device_id_type=MESH)
+
 
     mine = EDGE // 2 + func
     own_state = [pltpu.make_async_copy(chk.at[s], st.at[s, :, mine], own_sem.at[1 + s]) for s in range(2)]
@@ -153,7 +159,11 @@
         own_state[s].start()
     own_seeds = pltpu.make_async_copy(seeds, adj.at[:, :, pl.ds(EDGE, 32), :], own_sem.at[0])
     own_seeds.start()
-    pl.semaphore_wait(barrier, funcs + 1)
+    pl.semaphore_wait(barrier, funcs + 1 - bottom.astype(jnp.int32))
+
+    @pl.when(top)
+    def _():
+        pl.semaphore_signal(entered, inc=1, device_id=(up, func), device_id_type=MESH)
 
     gather = [
         [
@@ -190,15 +200,21 @@
     )
     for copy in gather[1]:
         copy.start()
-    for copy in halo:
-        copy.start()
+
+    def launch(pair):
+        pair[0].start()
+
+        @pl.when(jnp.logical_not(bottom))
+        def _():
+            pair[1].start()
+
+    launch(halo)
 
     def relay(s):
         own_state[s].wait()
         for copy in gather[s]:
             copy.wait_recv()
-        for copy in rims[s]:
-            copy.start()
+        launch(rims[s])
 
     relay(1)
     for copy in gather[0]:
@@ -209,44 +225,56 @@
         return lambda c, row: st[s, c, pl.ds(row // 2, 4), :, :].reshape(8, L)
 
     def part(g, carry):
-        def only(want, copies):
-            @pl.when(g == want)
+        above = (g == 0) != top
+
+        def arrive(pair):
+            @pl.when(above)
             def _():
-                for copy in copies:
-                    copy.wait_recv()
-
-        def region(below, above, low):
-            return jnp.where(g == 0, EDGE + low, EDGE + below), jnp.where(g == 0, EDGE + above, EDGE + low)
+                pair[1].wait_recv()
+
+            @pl.when(jnp.logical_not(above))
+            def _():
+                pair[0].wait_recv()
+
+        def region(deep, rim):
+            first, last = -deep, 32 + deep
+            low = jnp.where(top, jnp.where(g == 0, first, 32 - rim), jnp.where(g == 0, rim, first))
+            high = jnp.where(top, jnp.where(g == 0, 32 - rim, last), jnp.where(g == 0, last, rim))
+            return EDGE + low, EDGE + high
 
         def sections(s):
-            n = DEEP[s]
-            return lambda k: region(2 * k - n, 32 + n - 2 * k, 2 * k)
+            return lambda k: region(DEEP[s] - 2 * k, 2 * k)
 
         def stages(first):
-            return lambda place: region(-16 + 2 * (first + place), 48 - 2 * (first + place), 4 + 2 * (first + place))
-
-        only(0, (rims[1][1],))
-        only(1, (rims[1][0], halo[0]))
+            return lambda place: region(16 - 2 * (first + place), 4 + 2 * (first + place))
+
+        arrive(rims[1])
         forward(load(1), u0[1], fx[1], base[1], coef[1], sections(1))
 
         @pl.when(g == 0)
         def _():
             relay(0)
 
-        only(0, (halo[1],))
+        arrive(halo)
 
         def keep(f, c, row, v):
             fields[4][f, c, rowsat(row), :] = v
 
         backward(*fields[0:4], coef[1], stages(1), keep)
-        only(0, (rims[0][1],))
-        only(1, (rims[0][0],))
+        arrive(rims[0])
         forward(load(0), u0[0], fx[0], base[0], coef[0], sections(0))
 
         def finish(f, c, row, v):
             out[f, c, pl.ds(row - EDGE, 8), :] = v
 
         backward(*fields[4:8], coef[0], stages(5), finish)
+
+        @pl.when(jnp.logical_and(g == 0, bottom))
+        def _():
+            pl.semaphore_wait(entered, 1)
+            for pair in (halo, rims[1], rims[0]):
+                pair[1].start()
+
         return carry
 
     lax.fori_loop(0, 2, part, 0)
@@ -276,6 +304,7 @@
                 pltpu.SemaphoreType.DMA((2, 16)),
                 pltpu.SemaphoreType.DMA((6,)),
                 pltpu.SemaphoreType.DMA((6,)),
+                pltpu.SemaphoreType.REGULAR,
             ],
             compiler_params=pltpu.CompilerParams(
                 collective_id=0, has_side_effects=True, vmem_limit_bytes=16 * 2**20

time: 45.9 us -> 42 us (0.915)
  Pallas kernels: 43.4 us -> 39.4 us
    pallas_call x1, Pallas kernels: 43.4 us -> 39.4 us  [local(): pl.pallas_call(functools.partial(kernel, tiles, funcs), out_shape=jax.Sha...]
where the time goes in v3:
time: 42 us; the launch traced here: 41.8 us
  Pallas kernels  39.4 us (94%)
  local copies, waits for them, and re-layouts  2.34 us (6%)
    pallas_call x1, Pallas kernels, local(): pl.pallas_call(functools.partial(kernel, tiles, funcs), out_shape=jax.Sha...  39.4 us
    unnamed x5, local copies, waits for them, and re-layouts  2.34 us

profile of v3, /device:TPU:1, one launch (start us, length us, event | category | flops | bytes accessed | tf_op | source)
XLA Modules:
  0.0 41.8 jit_solution(11869339288456811146)
XLA Ops:
  0.0 0.0 copy-start
  0.0 0.9 %copy-done = f32[3,5,32,128]{3,2,1,0:T(8,128)S(1)} copy-done((f32[3,5,32,128]{3,2,1,0:T(8,128)S(1)}, f32[3,5,32,128]{3,2,1,0:T(8,128)}, u32[]{:S(2)}) %copy-start) | copy-done | bytes 245784
  0.9 0.0 copy-start.1
  0.9 0.7 %copy-done.1 = f32[2,5,2,128]{3,2,1,0:T(2,128)S(1)} copy-done((f32[2,5,2,128]{3,2,1,0:T(2,128)S(1)}, f32[2,5,2,128]{3,2,1,0:T(2,128)}, u32[]{:S(2)}) %copy-start.1) | copy-done | bytes 10264
  1.6 39.4 %shard_map.28 = f32[3,5,32,128]{3,2,1,0:T(8,128)S(1)} custom-call(f32[3,5,32,128]{3,2,1,0:T(8,128)S(1)} %copy-done, f32[2,5,2,128]{3,2,1,0:T(2,128)S(1)} %copy-done.1), custom_call_target="tpu_custom_call" | custom-call | tf_op jit(solution)/shard_map/pallas_call | solution.py:292
  41.1 0.7 %copy.4 = f32[3,5,32,128]{3,2,1,0:T(8,128)} copy(f32[3,5,32,128]{3,2,1,0:T(8,128)S(1)} %shard_map.28) | data formatting | bytes 491520
Async XLA Ops:
  0.0 0.9 %copy-start = (f32[3,5,32,128]{3,2,1,0:T(8,128)S(1)}, f32[3,5,32,128]{3,2,1,0:T(8,128)}, u32[]{:S(2)}) copy-start(f32[3,5,32,128]{3,2,1,0:T(8,128)} %seeds.1) | copy-start | bytes 737284
  0.9 0.7 %copy-start.1 = (f32[2,5,2,128]{3,2,1,0:T(2,128)S(1)}, f32[2,5,2,128]{3,2,1,0:T(2,128)}, u32[]{:S(2)}) copy-start(f32[2,5,2,128]{3,2,1,0:T(2,128)} %chk.1) | copy-start | bytes 30724

commit v4 on v3

--- a/solution.py
+++ b/solution.py
@@ -16,10 +16,16 @@
 MESH = pl.DeviceIdType.MESH
 
 
-def stencil_y(a):
-    far = pltpu.roll(a, 2 * NZ, 1) - pltpu.roll(a, L - 2 * NZ, 1)
-    near = pltpu.roll(a, L - NZ, 1) - pltpu.roll(a, NZ, 1)
-    return far + 8.0 * near
+def y_matrix():
+    gap = (lax.broadcasted_iota(jnp.int32, (L, L), 0) - lax.broadcasted_iota(jnp.int32, (L, L), 1) + L) % L
+    near = jnp.where(gap == NZ, 8.0, jnp.where(gap == L - NZ, -8.0, 0.0))
+    return near + jnp.where(gap == L - 2 * NZ, 1.0, jnp.where(gap == 2 * NZ, -1.0, 0.0))
+
+
+def along_y(v, mat):
+    high = v.astype(jnp.bfloat16)
+    low = (v - high.astype(jnp.float32)).astype(jnp.bfloat16)
+    return jnp.dot(high, mat, preferred_element_type=jnp.float32) + jnp.dot(low, mat, preferred_element_type=jnp.float32)
 
 
 def rowsat(row, shift=0):
@@ -30,14 +36,13 @@
     n = (hi - lo + 7) // 8
 
     def step(i, c):
-        for j in range(u):
-            f(jnp.minimum(lo + 8 * (u * i + j), hi - 8))
+        f([jnp.minimum(lo + 8 * (u * i + j), hi - 8) for j in range(u)])
         return c
 
     lax.fori_loop(0, (n + u - 1) // u, step, 0)
 
 
-def forward(load, u0, fx, base, coef, span):
+def forward(load, fx, base, coef, span, mat):
     scale = (0.5 * H / 12.0, 0.5 * H / 12.0, H / 12.0)
 
     def phase(k):
@@ -45,8 +50,6 @@
             r = rowsat(row)
             if k == 0:
                 u = [load(c, row) for c in range(5)]
-                for c in range(5):
-                    u0[c, r, :] = u[c]
             else:
                 src, cst, u = fx[k - 1], -scale[k - 1], []
                 for c in range(5):
@@ -65,75 +68,83 @@
             coef[k, 2, r, :] = vz
             coef[k, 3, r, :] = ep * inv
             coef[k, 4, r, :] = 0.5 * (kin2 * inv)
-            if k < 3:
-                fx[k][0, r, :] = mx
-                fx[k][1, r, :] = mx * vx + p
-                fx[k][2, r, :] = my * vx
-                fx[k][3, r, :] = mz * vx
-                fx[k][4, r, :] = ep * vx
-                fy = (my, mx * vy, my * vy + p, mz * vy, ep * vy)
-                start = u if k == 0 else [u0[c, r, :] for c in range(5)]
+            if k == 3:
+                return []
+            fx[k][0, r, :] = mx
+            fx[k][1, r, :] = mx * vx + p
+            fx[k][2, r, :] = my * vx
+            fx[k][3, r, :] = mz * vx
+            fx[k][4, r, :] = ep * vx
+            return [my, mx * vy, my * vy + p, mz * vy, ep * vy]
+
+        def tiles(rows):
+            fy = [flux for row in rows for flux in tile(row)]
+            if k == 3:
+                return
+            slope = scale[k] * along_y(jnp.concatenate(fy, axis=0), mat[...])
+            for j, row in enumerate(rows):
                 for c in range(5):
-                    base[k][c, r, :] = start[c] - scale[k] * stencil_y(fy[c])
+                    at = 8 * (5 * j + c)
+                    base[k][c, rowsat(row), :] = load(c, row) - slope[at : at + 8]
 
         lo, hi = span(k)
-        sweep(lo, hi, tile, 3)
+        sweep(lo, hi, tiles, 3)
 
     for k in range(4):
         phase(k)
 
 
-def pull(w, f, coef, row):
-    a, b, mid = [], [], []
+def pull(w, f, coef, row, b):
+    a = []
     for c in range(5):
-        v = w[f, c, rowsat(row), :]
-        mid.append(v)
         a.append(
             (w[f, c, rowsat(row, -2), :] - w[f, c, rowsat(row, 2), :])
             + 8.0 * (w[f, c, rowsat(row, 1), :] - w[f, c, rowsat(row, -1), :])
         )
-        b.append(stencil_y(v))
     vx, vy, vz, en, kin = coef
     s = a[1] * vx + a[2] * vy + a[3] * vz + a[4] * en
     q = b[1] * vx + b[2] * vy + b[3] * vz + b[4] * en
     e4 = a[4] * vx + b[4] * vy
     g = 0.4 * (a[1] + b[2] + e4)
-    out = (
+    return (
         kin * g - s * vx - q * vy,
         a[0] + s + a[1] * vx + b[1] * vy - g * vx,
         b[0] + q + a[2] * vx + b[2] * vy - g * vy,
         a[3] * vx + b[3] * vy - g * vz,
         e4 + g,
     )
-    return mid, out
-
-
-def backward(adj, w3, w2, w1, coef, span, store):
+
+
+def backward(adj, w3, w2, w1, coef, span, store, mat):
     near = 3.0 * H / 72.0
     plan = ((3, adj, w3, near), (2, w3, w2, near), (1, w2, w1, 2.0 * near), (0, w1, None, H / 72.0))
     for place, (k, src, dst, cst) in enumerate(plan):
 
-        def tile(row, k=k, src=src, dst=dst, cst=cst):
-            r = rowsat(row)
-            c5 = [coef[k, c, r, :] for c in range(5)]
-            for f in range(3):
-                mid, out = pull(src, f, c5, row)
-                for c in range(5):
-                    start = mid[c] if k == 3 else adj[f, c, r, :]
-                    if dst is not None:
-                        dst[f, c, r, :] = start + cst * out[c]
-                    else:
-                        mix = (w3[f, c, r, :] + mid[c]) + 2.0 * w2[f, c, r, :] - start
-                        store(f, c, row, mix * (1.0 / 3.0) + cst * out[c])
+        def tile(rows, k=k, src=src, dst=dst, cst=cst):
+            mid = [src[f, c, rowsat(row), :] for row in rows for f in range(3) for c in range(5)]
+            along = along_y(jnp.concatenate(mid, axis=0), mat[...])
+            for j, row in enumerate(rows):
+                r = rowsat(row)
+                c5 = [coef[k, c, r, :] for c in range(5)]
+                for f in range(3):
+                    first = 5 * (3 * j + f)
+                    out = pull(src, f, c5, row, [along[8 * (first + c) : 8 * (first + c) + 8] for c in range(5)])
+                    for c in range(5):
+                        start = mid[first + c] if k == 3 else adj[f, c, r, :]
+                        if dst is not None:
+                            dst[f, c, r, :] = start + cst * out[c]
+                        else:
+                            mix = (w3[f, c, r, :] + src[f, c, r, :]) + 2.0 * w2[f, c, r, :] - start
+                            store(f, c, row, mix * (1.0 / 3.0) + cst * out[c])
 
         lo, hi = span(place)
         sweep(lo, hi, tile, 1)
 
 
 def kernel(tiles, funcs, seeds, chk, out, *scratch):
-    u0, fx, base = scratch[0:2], (scratch[2:5], scratch[5:8]), (scratch[8:11], scratch[11:14])
-    coef, fields = scratch[14:16], scratch[16:24]
-    st, own_sem, g_send, g_recv, z_send, z_recv, entered = scratch[24:]
+    fx, base = (scratch[0:3], scratch[3:6]), (scratch[6:9], scratch[9:12])
+    coef, fields = scratch[12:14], scratch[14:22]
+    st, own_sem, g_send, g_recv, z_send, z_recv, entered, mat = scratch[22:]
     tile, func = lax.axis_index("tile"), lax.axis_index("func")
     up, down = lax.rem(tile + 1, tiles), lax.rem(tile + tiles - 1, tiles)
     adj = fields[0]
@@ -154,11 +165,12 @@
 
 
     mine = EDGE // 2 + func
-    own_state = [pltpu.make_async_copy(chk.at[s], st.at[s, :, mine], own_sem.at[1 + s]) for s in range(2)]
+    own_state = [pltpu.make_async_copy(chk.at[s], st.at[s, :, pl.ds(2 * mine, 2), :], own_sem.at[1 + s]) for s in range(2)]
     for s in (1, 0):
         own_state[s].start()
     own_seeds = pltpu.make_async_copy(seeds, adj.at[:, :, pl.ds(EDGE, 32), :], own_sem.at[0])
     own_seeds.start()
+    mat[...] = y_matrix().astype(jnp.bfloat16)
     pl.semaphore_wait(barrier, funcs + 1 - bottom.astype(jnp.int32))
 
     @pl.when(top)
@@ -169,7 +181,7 @@
         [
             pltpu.make_async_remote_copy(
                 src_ref=chk.at[s],
-                dst_ref=st.at[s, :, mine],
+                dst_ref=st.at[s, :, pl.ds(2 * mine, 2), :],
                 send_sem=g_send.at[s, d],
                 recv_sem=g_recv.at[s, d],
                 device_id=(tile, peer(d)),
@@ -189,8 +201,8 @@
     lo, hi = EDGE // 2, EDGE // 2 + 16
     rims = [
         (
-            across(st.at[s, :, pl.ds(hi - n, n)], st.at[s, :, pl.ds(lo - n, n)], 2 + 2 * s, up),
-            across(st.at[s, :, pl.ds(lo, n)], st.at[s, :, pl.ds(hi, n)], 3 + 2 * s, down),
+            across(st.at[s, :, pl.ds(2 * (hi - n), 2 * n), :], st.at[s, :, pl.ds(2 * (lo - n), 2 * n), :], 2 + 2 * s, up),
+            across(st.at[s, :, pl.ds(2 * lo, 2 * n), :], st.at[s, :, pl.ds(2 * hi, 2 * n), :], 3 + 2 * s, down),
         )
         for s, n in enumerate((DEEP[0] // 2, DEEP[1] // 2))
     ]
@@ -222,7 +234,7 @@
     own_seeds.wait()
 
     def load(s):
-        return lambda c, row: st[s, c, pl.ds(row // 2, 4), :, :].reshape(8, L)
+        return lambda c, row: st[s, c, rowsat(row), :]
 
     def part(g, carry):
         above = (g == 0) != top
@@ -249,7 +261,7 @@
             return lambda place: region(16 - 2 * (first + place), 4 + 2 * (first + place))
 
         arrive(rims[1])
-        forward(load(1), u0[1], fx[1], base[1], coef[1], sections(1))
+        forward(load(1), fx[1], base[1], coef[1], sections(1), mat)
 
         @pl.when(g == 0)
         def _():
@@ -260,14 +272,14 @@
         def keep(f, c, row, v):
             fields[4][f, c, rowsat(row), :] = v
 
-        backward(*fields[0:4], coef[1], stages(1), keep)
+        backward(*fields[0:4], coef[1], stages(1), keep, mat)
         arrive(rims[0])
-        forward(load(0), u0[0], fx[0], base[0], coef[0], sections(0))
+        forward(load(0), fx[0], base[0], coef[0], sections(0), mat)
 
         def finish(f, c, row, v):
             out[f, c, pl.ds(row - EDGE, 8), :] = v
 
-        backward(*fields[4:8], coef[0], stages(5), finish)
+        backward(*fields[4:8], coef[0], stages(5), finish, mat)
 
         @pl.when(jnp.logical_and(g == 0, bottom))
         def _():
@@ -294,17 +306,18 @@
             out_shape=jax.ShapeDtypeStruct(seeds.shape, jnp.float32),
             in_specs=[pl.BlockSpec(memory_space=pltpu.HBM)] * 2,
             out_specs=pl.BlockSpec(memory_space=pltpu.VMEM),
-            scratch_shapes=[state] * 14
+            scratch_shapes=[state] * 12
             + [pltpu.VMEM((4, 5, ROWS, L), jnp.float32)] * 2
             + [field] * 8
             + [
-                pltpu.VMEM((2, 5, ROWS // 2, 2, L), jnp.float32),
+                pltpu.VMEM((2, 5, ROWS, L), jnp.float32),
                 pltpu.SemaphoreType.DMA((3,)),
                 pltpu.SemaphoreType.DMA((2, 16)),
                 pltpu.SemaphoreType.DMA((2, 16)),
                 pltpu.SemaphoreType.DMA((6,)),
                 pltpu.SemaphoreType.DMA((6,)),
                 pltpu.SemaphoreType.REGULAR,
+                pltpu.VMEM((L, L), jnp.bfloat16),
             ],
             compiler_params=pltpu.CompilerParams(
                 collective_id=0, has_side_effects=True, vmem_limit_bytes=16 * 2**20

time: 42 us -> 42.3 us (level)
  no operation moved by 1% of the time
where the time goes in v4:
time: 42.3 us; the launch traced here: 42.1 us
  Pallas kernels  39.8 us (94%)
  local copies, waits for them, and re-layouts  2.34 us (6%)
    pallas_call x1, Pallas kernels, local(): pl.pallas_call(functools.partial(kernel, tiles, funcs), out_shape=jax.Sha...  39.8 us
    unnamed x5, local copies, waits for them, and re-layouts  2.34 us

profile of v4, /device:TPU:1, one launch (start us, length us, event | category | flops | bytes accessed | tf_op | source)
XLA Modules:
  0.0 42.1 jit_solution(15522023673857371774)
XLA Ops:
  0.0 0.0 copy-start
  0.0 0.9 %copy-done = f32[3,5,32,128]{3,2,1,0:T(8,128)S(1)} copy-done((f32[3,5,32,128]{3,2,1,0:T(8,128)S(1)}, f32[3,5,32,128]{3,2,1,0:T(8,128)}, u32[]{:S(2)}) %copy-start) | copy-done | bytes 245784
  0.9 0.0 copy-start.1
  0.9 0.7 %copy-done.1 = f32[2,5,2,128]{3,2,1,0:T(2,128)S(1)} copy-done((f32[2,5,2,128]{3,2,1,0:T(2,128)S(1)}, f32[2,5,2,128]{3,2,1,0:T(2,128)}, u32[]{:S(2)}) %copy-start.1) | copy-done | bytes 10264
  1.6 39.8 %shard_map.28 = f32[3,5,32,128]{3,2,1,0:T(8,128)S(1)} custom-call(f32[3,5,32,128]{3,2,1,0:T(8,128)S(1)} %copy-done, f32[2,5,2,128]{3,2,1,0:T(2,128)S(1)} %copy-done.1), custom_call_target="tpu_custom_call" | custom-call | tf_op jit(solution)/shard_map/pallas_call | solution.py:304
  41.4 0.7 %copy.4 = f32[3,5,32,128]{3,2,1,0:T(8,128)} copy(f32[3,5,32,128]{3,2,1,0:T(8,128)S(1)} %shard_map.28) | data formatting | bytes 491520
Async XLA Ops:
  0.0 0.9 %copy-start = (f32[3,5,32,128]{3,2,1,0:T(8,128)S(1)}, f32[3,5,32,128]{3,2,1,0:T(8,128)}, u32[]{:S(2)}) copy-start(f32[3,5,32,128]{3,2,1,0:T(8,128)} %seeds.1) | copy-start | bytes 737284
  0.9 0.7 %copy-start.1 = (f32[2,5,2,128]{3,2,1,0:T(2,128)S(1)}, f32[2,5,2,128]{3,2,1,0:T(2,128)}, u32[]{:S(2)}) copy-start(f32[2,5,2,128]{3,2,1,0:T(2,128)} %chk.1) | copy-start | bytes 30724

commit v5 on v4

--- a/solution.py
+++ b/solution.py
@@ -28,6 +28,12 @@
     return jnp.dot(high, mat, preferred_element_type=jnp.float32) + jnp.dot(low, mat, preferred_element_type=jnp.float32)
 
 
+def rolled_y(a):
+    far = pltpu.roll(a, 2 * NZ, 1) - pltpu.roll(a, L - 2 * NZ, 1)
+    near = pltpu.roll(a, L - NZ, 1) - pltpu.roll(a, NZ, 1)
+    return far + 8.0 * near
+
+
 def rowsat(row, shift=0):
     return pl.ds(row + shift, 8)
 
@@ -42,7 +48,7 @@
     lax.fori_loop(0, (n + u - 1) // u, step, 0)
 
 
-def forward(load, fx, base, coef, span, mat):
+def forward(load, fx, base, coef, span):
     scale = (0.5 * H / 12.0, 0.5 * H / 12.0, H / 12.0)
 
     def phase(k):
@@ -78,14 +84,9 @@
             return [my, mx * vy, my * vy + p, mz * vy, ep * vy]
 
         def tiles(rows):
-            fy = [flux for row in rows for flux in tile(row)]
-            if k == 3:
-                return
-            slope = scale[k] * along_y(jnp.concatenate(fy, axis=0), mat[...])
-            for j, row in enumerate(rows):
-                for c in range(5):
-                    at = 8 * (5 * j + c)
-                    base[k][c, rowsat(row), :] = load(c, row) - slope[at : at + 8]
+            for row in rows:
+                for c, flux in enumerate(tile(row)):
+                    base[k][c, rowsat(row), :] = load(c, row) - scale[k] * rolled_y(flux)
 
         lo, hi = span(k)
         sweep(lo, hi, tiles, 3)
@@ -138,7 +139,7 @@
                             store(f, c, row, mix * (1.0 / 3.0) + cst * out[c])
 
         lo, hi = span(place)
-        sweep(lo, hi, tile, 1)
+        sweep(lo, hi, tile, 4)
 
 
 def kernel(tiles, funcs, seeds, chk, out, *scratch):
@@ -261,7 +262,7 @@
             return lambda place: region(16 - 2 * (first + place), 4 + 2 * (first + place))
 
         arrive(rims[1])
-        forward(load(1), fx[1], base[1], coef[1], sections(1), mat)
+        forward(load(1), fx[1], base[1], coef[1], sections(1))
 
         @pl.when(g == 0)
         def _():
@@ -274,7 +275,7 @@
 
         backward(*fields[0:4], coef[1], stages(1), keep, mat)
         arrive(rims[0])
-        forward(load(0), fx[0], base[0], coef[0], sections(0), mat)
+        forward(load(0), fx[0], base[0], coef[0], sections(0))
 
         def finish(f, c, row, v):
             out[f, c, pl.ds(row - EDGE, 8), :] = v

time: 42.3 us -> 41.3 us (0.976)
  Pallas kernels: 39.8 us -> 38.7 us
    pallas_call x1, Pallas kernels: 39.8 us -> 38.7 us  [local(): pl.pallas_call(functools.partial(kernel, tiles, funcs), out_shape=jax.Sha...]
where the time goes in v5:
time: 41.3 us; the launch traced here: 41.1 us
  Pallas kernels  38.7 us (94%)
  local copies, waits for them, and re-layouts  2.34 us (6%)
    pallas_call x1, Pallas kernels, local(): pl.pallas_call(functools.partial(kernel, tiles, funcs), out_shape=jax.Sha...  38.7 us
    unnamed x5, local copies, waits for them, and re-layouts  2.34 us

profile of v5, /device:TPU:1, one launch (start us, length us, event | category | flops | bytes accessed | tf_op | source)
XLA Modules:
  0.0 41.1 jit_solution(3843534947861503102)
XLA Ops:
  0.0 0.0 copy-start
  0.0 0.9 %copy-done = f32[3,5,32,128]{3,2,1,0:T(8,128)S(1)} copy-done((f32[3,5,32,128]{3,2,1,0:T(8,128)S(1)}, f32[3,5,32,128]{3,2,1,0:T(8,128)}, u32[]{:S(2)}) %copy-start) | copy-done | bytes 245784
  0.9 0.0 copy-start.1
  0.9 0.7 %copy-done.1 = f32[2,5,2,128]{3,2,1,0:T(2,128)S(1)} copy-done((f32[2,5,2,128]{3,2,1,0:T(2,128)S(1)}, f32[2,5,2,128]{3,2,1,0:T(2,128)}, u32[]{:S(2)}) %copy-start.1) | copy-done | bytes 10264
  1.6 38.7 %shard_map.28 = f32[3,5,32,128]{3,2,1,0:T(8,128)S(1)} custom-call(f32[3,5,32,128]{3,2,1,0:T(8,128)S(1)} %copy-done, f32[2,5,2,128]{3,2,1,0:T(2,128)S(1)} %copy-done.1), custom_call_target="tpu_custom_call" | custom-call | tf_op jit(solution)/shard_map/pallas_call | solution.py:305
  40.4 0.7 %copy.4 = f32[3,5,32,128]{3,2,1,0:T(8,128)} copy(f32[3,5,32,128]{3,2,1,0:T(8,128)S(1)} %shard_map.28) | data formatting | bytes 491520
Async XLA Ops:
  0.0 0.9 %copy-start = (f32[3,5,32,128]{3,2,1,0:T(8,128)S(1)}, f32[3,5,32,128]{3,2,1,0:T(8,128)}, u32[]{:S(2)}) copy-start(f32[3,5,32,128]{3,2,1,0:T(8,128)} %seeds.1) | copy-start | bytes 737284
  0.9 0.7 %copy-start.1 = (f32[2,5,2,128]{3,2,1,0:T(2,128)S(1)}, f32[2,5,2,128]{3,2,1,0:T(2,128)}, u32[]{:S(2)}) copy-start(f32[2,5,2,128]{3,2,1,0:T(2,128)} %chk.1) | copy-start | bytes 30724

commit v6 on v5

--- a/solution.py
+++ b/solution.py
@@ -321,7 +321,7 @@
                 pltpu.VMEM((L, L), jnp.bfloat16),
             ],
             compiler_params=pltpu.CompilerParams(
-                collective_id=0, has_side_effects=True, vmem_limit_bytes=16 * 2**20
+                collective_id=0, has_side_effects=True, vmem_limit_bytes=60_000_000
             ),
         )(seeds, checkpoints)
 

time: 41.3 us -> 41.4 us (level)
  Pallas kernels: 38.7 us -> 39.6 us
  local copies, waits for them, and re-layouts: 2.34 us -> 1.65 us
    pallas_call x1, Pallas kernels: 38.7 us -> 39.6 us  [local(): pl.pallas_call(functools.partial(kernel, tiles, funcs), out_shape=jax.Sha...]
    unnamed x5 -> x1, local copies, waits for them, and re-layouts: 2.34 us -> 1.65 us
where the time goes in v6:
time: 41.4 us; the launch traced here: 41.3 us
  Pallas kernels  39.6 us (96%)
  local copies, waits for them, and re-layouts  1.65 us (4%)
    pallas_call x1, Pallas kernels, local(): pl.pallas_call(functools.partial(kernel, tiles, funcs), out_shape=jax.Sha...  39.6 us
    unnamed x1, local copies, waits for them, and re-layouts  1.65 us

profile of v6, /device:TPU:1, one launch (start us, length us, event | category | flops | bytes accessed | tf_op | source)
XLA Modules:
  0.0 41.3 jit_solution(7137380998613804171)
XLA Ops:
  0.0 39.6 %shard_map.28 = f32[3,5,32,128]{3,2,1,0:T(8,128)} custom-call(f32[3,5,32,128]{3,2,1,0:T(8,128)} %seeds.1, f32[2,5,2,128]{3,2,1,0:T(2,128)} %chk.1), custom_call_target="tpu_custom_call" | custom-call | tf_op jit(solution)/shard_map/pallas_call | solution.py:305
  39.6 1.7 %copy.4 = f32[3,5,32,128]{3,2,1,0:T(8,128)} copy(f32[3,5,32,128]{3,2,1,0:T(8,128)} %shard_map.28) | data formatting | bytes 491520

commit v7 on v5

--- a/solution.py
+++ b/solution.py
@@ -211,8 +211,8 @@
         across(seeds.at[:, :, pl.ds(16, 16), :], adj.at[:, :, pl.ds(EDGE - 16, 16), :], 0, up),
         across(seeds.at[:, :, pl.ds(0, 16), :], adj.at[:, :, pl.ds(EDGE + 32, 16), :], 1, down),
     )
-    for copy in gather[1]:
-        copy.start()
+    for d in sorted(range(1, funcs), key=lambda d: -min(d, funcs - d)):
+        gather[1][d - 1].start()
 
     def launch(pair):
         pair[0].start()

time: 41.3 us -> 41.3 us (level)
  no operation moved by 1% of the time
where the time goes in v7:
time: 41.3 us; the launch traced here: 41.1 us
  Pallas kernels  38.7 us (94%)
  local copies, waits for them, and re-layouts  2.34 us (6%)
    pallas_call x1, Pallas kernels, local(): pl.pallas_call(functools.partial(kernel, tiles, funcs), out_shape=jax.Sha...  38.7 us
    unnamed x5, local copies, waits for them, and re-layouts  2.34 us

profile of v7, /device:TPU:1, one launch (start us, length us, event | category | flops | bytes accessed | tf_op | source)
XLA Modules:
  0.0 41.1 jit_solution(13126565205570922324)
XLA Ops:
  0.0 0.0 copy-start
  0.0 0.9 %copy-done = f32[3,5,32,128]{3,2,1,0:T(8,128)S(1)} copy-done((f32[3,5,32,128]{3,2,1,0:T(8,128)S(1)}, f32[3,5,32,128]{3,2,1,0:T(8,128)}, u32[]{:S(2)}) %copy-start) | copy-done | bytes 245784
  0.9 0.0 copy-start.1
  0.9 0.7 %copy-done.1 = f32[2,5,2,128]{3,2,1,0:T(2,128)S(1)} copy-done((f32[2,5,2,128]{3,2,1,0:T(2,128)S(1)}, f32[2,5,2,128]{3,2,1,0:T(2,128)}, u32[]{:S(2)}) %copy-start.1) | copy-done | bytes 10264
  1.6 38.7 %shard_map.28 = f32[3,5,32,128]{3,2,1,0:T(8,128)S(1)} custom-call(f32[3,5,32,128]{3,2,1,0:T(8,128)S(1)} %copy-done, f32[2,5,2,128]{3,2,1,0:T(2,128)S(1)} %copy-done.1), custom_call_target="tpu_custom_call" | custom-call | tf_op jit(solution)/shard_map/pallas_call | solution.py:305
  40.4 0.7 %copy.4 = f32[3,5,32,128]{3,2,1,0:T(8,128)} copy(f32[3,5,32,128]{3,2,1,0:T(8,128)S(1)} %shard_map.28) | data formatting | bytes 491520
Async XLA Ops:
  0.0 0.9 %copy-start = (f32[3,5,32,128]{3,2,1,0:T(8,128)S(1)}, f32[3,5,32,128]{3,2,1,0:T(8,128)}, u32[]{:S(2)}) copy-start(f32[3,5,32,128]{3,2,1,0:T(8,128)} %seeds.1) | copy-start | bytes 737284
  0.9 0.7 %copy-start.1 = (f32[2,5,2,128]{3,2,1,0:T(2,128)S(1)}, f32[2,5,2,128]{3,2,1,0:T(2,128)}, u32[]{:S(2)}) copy-start(f32[2,5,2,128]{3,2,1,0:T(2,128)} %chk.1) | copy-start | bytes 30724
